TPU v7x, 512 devices: a whole 4x8x8 slice. The times are simulated.
512 devices in a mesh: dp: 16 (over y, core), seq: 32 (over x, z).
Axes of the slice: x: 4, y: 8, z: 8, core: 2. Of those that a mesh axis runs over, the one named last changes fastest.
Arguments:
- queries: bfloat16 [131072, 4096], P(('dp', 'seq')), parts along dimension 0, may hold values from -6 to 6
- keys: bfloat16 [131072, 1024], P(('dp', 'seq')), parts along dimension 0, may hold values from -6 to 6
- values: bfloat16 [131072, 1024], P(('dp', 'seq')), parts along dimension 0, may hold values from -6 to 6
- lengths: int32 [512], P('dp'), parts along dimension 0, may hold values from 1 to 1024, 8192 in all
- span_order: int32 [2048], P('dp'), parts along dimension 0, may hold values from 0 to 127, each once
Outputs:
- attended: bfloat16 [131072, 4096], P(('dp', 'seq')), parts along dimension 0
There are 16 independent parts, one for each index of `dp`. A program takes and returns all parts, laid end to end along the dimension named above; each array names one. Nothing has to cross between parts.
Inputs may be any that keep to these rules, and one draw needn't show every extreme that they name: The lengths of one packed sequence sum to 8192; the longest is exactly 1024. A permutation of the 128 spans: balanced row b * 64 + i holds loader token span_order[b] * 64 + i.
All inputs are finite; a program needn't handle non-finite values.
Results may differ from a plain program's by a relative error of at most 0.0034.
Values may be sent and summed in bfloat16 or wider, within the bound.
A program may use at most 64 MiB of HBM per device.

v0:
```python
import jax
import jax.numpy as jnp
from jax import lax
from jax.sharding import PartitionSpec as P

HEADS = 32
KV_HEADS = 8
HEAD_DIM = 128
BLOCK = 64
DOC_MOST = 1024
QBLOCK = 512


def doc_numbers(lengths, places):
    doc_ends = jnp.cumsum(lengths)
    return jnp.sum((doc_ends[None, :] <= places[:, None]).astype(jnp.int32), axis=1)


def attend(head_queries, key_sets, value_sets, doc_ids):
    total_rows = head_queries.shape[0]
    heads_here = head_queries.shape[1]
    shared = key_sets.shape[1] == 1
    pad_keys = jnp.concatenate(
        [jnp.zeros((DOC_MOST,) + key_sets.shape[1:], key_sets.dtype), key_sets], 0
    )
    pad_values = jnp.concatenate(
        [jnp.zeros((DOC_MOST,) + value_sets.shape[1:], value_sets.dtype), value_sets], 0
    )
    pad_docs = jnp.concatenate([jnp.full((DOC_MOST,), -1, jnp.int32), doc_ids], 0)
    scale_factor = HEAD_DIM ** (-0.5)

    def one_block(block_index):
        row_start = block_index * QBLOCK
        query_block = lax.dynamic_slice_in_dim(head_queries, row_start, QBLOCK, 0)
        key_block = lax.dynamic_slice_in_dim(pad_keys, row_start, QBLOCK + DOC_MOST, 0)
        value_block = lax.dynamic_slice_in_dim(pad_values, row_start, QBLOCK + DOC_MOST, 0)
        query_docs = lax.dynamic_slice_in_dim(pad_docs, row_start + DOC_MOST, QBLOCK, 0)
        key_docs = lax.dynamic_slice_in_dim(pad_docs, row_start, QBLOCK + DOC_MOST, 0)
        query_pos = row_start + jnp.arange(QBLOCK, dtype=jnp.int32)
        key_pos = row_start - DOC_MOST + jnp.arange(QBLOCK + DOC_MOST, dtype=jnp.int32)
        allowed = (query_docs[:, None] == key_docs[None, :]) & (
            key_pos[None, :] <= query_pos[:, None]
        )
        scores = jnp.einsum(
            "qgd,kd->gqk", query_block, key_block[:, 0], preferred_element_type=jnp.float32
        )
        scores = jnp.where(allowed[None], scores * scale_factor, -jnp.inf)
        row_top = jnp.max(scores, axis=-1, keepdims=True)
        weights = jnp.exp(scores - row_top)
        row_total = jnp.sum(weights, axis=-1, keepdims=True)
        rounded = weights.astype(jnp.bfloat16)
        mixed_rows = jnp.einsum(
            "gqk,kd->qgd", rounded, value_block[:, 0], preferred_element_type=jnp.float32
        )
        return (mixed_rows / jnp.transpose(row_total, (1, 0, 2))).astype(jnp.bfloat16)

    blocks = lax.map(one_block, jnp.arange(total_rows // QBLOCK, dtype=jnp.int32))
    return blocks.reshape(total_rows, heads_here * HEAD_DIM)


def shards(queries, keys, values, lengths, span_order):
    seq_devices = lax.axis_size("seq")
    rows_here = queries.shape[0]
    total_rows = rows_here * seq_devices
    nchunk = span_order.shape[0]
    heads_here = HEADS // seq_devices
    group_size = HEADS // KV_HEADS
    inverse = (
        jnp.zeros((nchunk,), jnp.int32).at[span_order].set(jnp.arange(nchunk, dtype=jnp.int32))
    )

    def to_loader(array):
        return array.reshape(nchunk, BLOCK, -1)[inverse].reshape(total_rows, -1)

    wide_keys = jnp.repeat(
        keys.reshape(rows_here, KV_HEADS, 1, HEAD_DIM), group_size, axis=2
    ).reshape(rows_here, HEADS * HEAD_DIM)
    wide_values = jnp.repeat(
        values.reshape(rows_here, KV_HEADS, 1, HEAD_DIM), group_size, axis=2
    ).reshape(rows_here, HEADS * HEAD_DIM)
    head_q, head_k, head_v = (
        lax.all_to_all(queries, "seq", split_axis=1, concat_axis=0, tiled=True),
        lax.all_to_all(wide_keys, "seq", split_axis=1, concat_axis=0, tiled=True),
        lax.all_to_all(wide_values, "seq", split_axis=1, concat_axis=0, tiled=True),
    )
    key_sets = to_loader(head_k).reshape(total_rows, heads_here, HEAD_DIM)
    value_sets = to_loader(head_v).reshape(total_rows, heads_here, HEAD_DIM)
    loader_queries = to_loader(head_q).reshape(total_rows, heads_here, HEAD_DIM)
    doc_ids = doc_numbers(lengths, jnp.arange(total_rows, dtype=jnp.int32))
    loader_out = attend(loader_queries, key_sets, value_sets, doc_ids)
    balanced_out = loader_out.reshape(nchunk, BLOCK, -1)[span_order].reshape(total_rows, -1)
    return lax.all_to_all(balanced_out, "seq", split_axis=0, concat_axis=1, tiled=True)


def solution(mesh):
    placed = (
        P(("dp", "seq"), None),
        P(("dp", "seq"), None),
        P(("dp", "seq"), None),
        P("dp"),
        P("dp"),
    )
    return jax.shard_map(
        shards, mesh=mesh, in_specs=placed, out_specs=P(("dp", "seq"), None), check_vma=False
    )
```

profile of v0, /device:TPU:56, one launch (start us, length us, event | category | flops | bytes accessed | tf_op | source)
XLA Modules:
  0.0 366.4 jit_solution(15063499089256534793)
XLA Ops:
  2.9 13.2 %all-to-all-start.1 = ((bf16[256,32,128]{2,0,1:T(8,128)(2,1)}), bf16[256,32,128]{2,0,1:T(8,128)(2,1)S(1)}, u32[]{:S(2)}, u32[]{:S(2)}) async-start(bf16[256,32,128]{2,0,1:T(8,128)(2,1)} %bitcast.15), calls=%async_computation.1 | async-start | bytes 4194304 | tf_op jit(solution)/shard_map/all_to_all | solution.py:83
  17.3 48.9 %all-to-all-done.1 = bf16[256,32,128]{2,0,1:T(8,128)(2,1)S(1)} async-done(((bf16[256,32,128]{2,0,1:T(8,128)(2,1)}), bf16[256,32,128]{2,0,1:T(8,128)(2,1)S(1)}, u32[]{:S(2)}, u32[]{:S(2)}) %all-to-all-start.1) | async-done | bytes 2097184 | tf_op jit(solution)/shard_map/all_to_all | solution.py:83
  68.0 6.3 %all-to-all-start = ((bf16[256,32,128]{2,0,1:T(8,128)(2,1)}), bf16[256,32,128]{2,0,1:T(8,128)(2,1)}, u32[]{:S(2)}, u32[]{:S(2)}) async-start(bf16[256,32,128]{2,0,1:T(8,128)(2,1)} %bitcast.10), calls=%async_computation | async-start | bytes 4194304 | tf_op jit(solution)/shard_map/all_to_all | solution.py:84
  74.3 4.1 %copy.22 = bf16[256,4096]{0,1:T(8,128)(2,1)} copy(bf16[256,4096]{1,0:T(8,128)(2,1)} %param.7) | data formatting | bytes 4194304 | tf_op args[0]
  78.4 45.6 %all-to-all-done = bf16[256,32,128]{2,0,1:T(8,128)(2,1)} async-done(((bf16[256,32,128]{2,0,1:T(8,128)(2,1)}), bf16[256,32,128]{2,0,1:T(8,128)(2,1)}, u32[]{:S(2)}, u32[]{:S(2)}) %all-to-all-start) | async-done | bytes 2097184 | tf_op jit(solution)/shard_map/all_to_all | solution.py:84
  124.1 6.4 %all-to-all-start.2 = ((bf16[256,32,128]{0,2,1:T(8,128)(2,1)}), bf16[256,32,128]{0,2,1:T(8,128)(2,1)}, u32[]{:S(2)}, u32[]{:S(2)}) async-start(bf16[256,32,128]{0,2,1:T(8,128)(2,1)} %bitcast.87), calls=%async_computation.2 | async-start | bytes 4194304 | tf_op jit(solution)/shard_map/all_to_all | solution.py:82
  134.2 2.5 gather_fusion
  136.7 2.7 concatenate.11
  141.4 38.7 %all-to-all-done.2 = bf16[256,32,128]{0,2,1:T(8,128)(2,1)} async-done(((bf16[256,32,128]{0,2,1:T(8,128)(2,1)}), bf16[256,32,128]{0,2,1:T(8,128)(2,1)}, u32[]{:S(2)}, u32[]{:S(2)}) %all-to-all-start.2) | async-done | bytes 2097184 | tf_op jit(solution)/shard_map/all_to_all | solution.py:82
  180.1 3.2 copy.23
  183.3 2.2 gather_fusion.2
  185.5 115.3 %while.12 = (s32[]{:T(128)}, bf16[16,512,1,128]{3,1,0,2:T(8,128)(2,1)}, s32[16]{0:T(128)S(1)}, bf16[9216,1,128]{2,0,1:T(8,128)(2,1)}, s32[9216]{0:T(1024)S(1)}, ...) while((s32[]{:T(128)}, ...), condition=%wide.region_6.7_spmd, body=%wide.region_3.6_spmd.sunk | while | flops 410649600 | bytes 11062070 | solution.py:57
  187.1 2.7 fusion.39
  194.3 2.7 fusion.39
  201.5 2.7 fusion.39
  208.7 2.7 fusion.39
  215.9 2.7 fusion.39
  223.1 2.7 fusion.39
  230.3 2.7 fusion.39
  237.5 2.7 fusion.39
  244.7 2.7 fusion.39
  251.9 2.7 fusion.39
  259.1 2.7 fusion.39
  266.4 2.7 fusion.39
  273.6 2.7 fusion.39
  280.8 2.7 fusion.39
  288.0 2.7 fusion.39
  295.2 2.7 fusion.39
  300.9 2.5 gather_fusion.3
  303.4 56.9 %all_to_all.67 = bf16[32,256,128]{2,1,0:T(8,128)(2,1)} all-to-all(bf16[32,256,128]{2,1,0:T(8,128)(2,1)S(1)} %bitcast.91), channel_id=1, replica_groups=mesh['dp'=16,'seq'=32] {'seq'}, dimensions={0} | all-to-all | bytes 4194304 | tf_op jit(solution)/shard_map/all_to_all | solution.py:92
  360.3 3.3 copy.25
  363.6 2.9 copy.26
  (169 shorter events, 72.2 us)
Async XLA Ops:
  0.0 1.0 copy-start
  2.9 63.2 %all-to-all-start.1 = ((bf16[256,32,128]{2,0,1:T(8,128)(2,1)}), bf16[256,32,128]{2,0,1:T(8,128)(2,1)S(1)}, u32[]{:S(2)}, u32[]{:S(2)}) async-start(bf16[256,32,128]{2,0,1:T(8,128)(2,1)} %bitcast.15), calls=%async_computation.1 | async-start | bytes 4194304 | tf_op jit(solution)/shard_map/all_to_all | solution.py:83
  68.0 56.0 %all-to-all-start = ((bf16[256,32,128]{2,0,1:T(8,128)(2,1)}), bf16[256,32,128]{2,0,1:T(8,128)(2,1)}, u32[]{:S(2)}, u32[]{:S(2)}) async-start(bf16[256,32,128]{2,0,1:T(8,128)(2,1)} %bitcast.10), calls=%async_computation | async-start | bytes 4194304 | tf_op jit(solution)/shard_map/all_to_all | solution.py:84
  124.0 6.4 %copy-start.1 = (s32[32]{0:T(128)S(1)}, s32[32]{0:T(128)}, u32[]{:S(2)}) copy-start(s32[32]{0:T(128)} %param.10) | copy-start | bytes 388
  124.0 6.7 %copy-start.2 = (s32[128]{0:T(128)S(1)}, s32[128]{0:T(128)}, u32[]{:S(2)}) copy-start(s32[128]{0:T(128)} %param.11) | copy-start | bytes 1540
  124.1 56.1 %all-to-all-start.2 = ((bf16[256,32,128]{0,2,1:T(8,128)(2,1)}), bf16[256,32,128]{0,2,1:T(8,128)(2,1)}, u32[]{:S(2)}, u32[]{:S(2)}) async-start(bf16[256,32,128]{0,2,1:T(8,128)(2,1)} %bitcast.87), calls=%async_computation.2 | async-start | bytes 4194304 | tf_op jit(solution)/shard_map/all_to_all | solution.py:82
where the time goes:
time: 369 us; the launch traced here: 366 us
  waiting for transfers between devices  133 us (36%)
  matrix products  69.9 us (19%)
  local copies, waits for them, and re-layouts  60.3 us (16%)
  blocking collectives  56.9 us (15%)
  starting transfers between devices  25.8 us (7%)
  loops' own time  11.6 us (3%)
  other arithmetic  8.5 us (2%)
    all_to_all x1, blocking collectives, shards(): lax.all_to_all(balanced_out, 'seq', split_axis=0, concat_axis=1, tiled=True)  56.9 us
    all_to_all x1, waiting for transfers between devices, shards(): lax.all_to_all(wide_keys, 'seq', split_axis=1, concat_axis=0, tiled=True)  48.9 us
    all_to_all x1, waiting for transfers between devices, shards(): lax.all_to_all(wide_values, 'seq', split_axis=1, concat_axis=0, tiled=True)  45.6 us
    dot_general x16, matrix products, one_block(): jnp.einsum('qgd,kd->gqk', query_block, key_block[:, 0], preferred_element...  43.1 us
    all_to_all x1, waiting for transfers between devices, shards(): lax.all_to_all(queries, 'seq', split_axis=1, concat_axis=0, tiled=True)  38.7 us
    dot_general x16, matrix products, one_block(): jnp.einsum('gqk,kd->qgd', rounded, value_block[:, 0], preferred_element_t...  26.9 us
    all_to_all x1, starting transfers between devices, shards(): lax.all_to_all(wide_keys, 'seq', split_axis=1, concat_axis=0, tiled=True)  13.2 us
    dynamic_update_slice x32, local copies, waits for them, and re-layouts, attend(): lax.map(one_block, jnp.arange(total_rows // QBLOCK, dtype=jnp.int32))  12.6 us
  transfers between devices with their start and end apart: 3, of which 3 were waited for; matrix products, arithmetic and copies ran while one was open for 4% of the time, Pallas kernels for 0%

commit v1 on v0

v1 whole, which is shorter than its diff:
```python
import math

import jax
import jax.numpy as jnp
from jax import lax
from jax.experimental import pallas as pl
from jax.experimental.pallas import tpu as pltpu
from jax.sharding import PartitionSpec as P

HEADS = 32
KV_HEADS = 8
HEAD_DIM = 128
BLOCK = 64
NX = 4
NZ = 8
ROWS = 256
SPANS = ROWS // BLOCK
GROUP = HEADS // KV_HEADS
KVH = KV_HEADS // NX
QW = HEADS * HEAD_DIM // NX
GW = GROUP * HEAD_DIM
TOKENS = NX * NZ * ROWS
NSPAN = TOKENS // BLOCK
PAD = 17
WIN = 18
UNITS = NX * SPANS
HALF = UNITS // 2
NDOC = 32
FORWARDS = 10
SCALE = HEAD_DIM**-0.5 * math.log2(math.e)


def body(
    lengths, order, places, queries, keys, values, out,
    kv_first, kv_second, loader_k, loader_v, q_buf, o_buf, starts,
    x_send, x_recv, q_send, q_recv, z_send, z_recv, o_send, o_recv,
):
    me = lax.axis_index("seq")
    x = me // NZ
    z = lax.rem(me, NZ)

    def at_x(offset):
        return lax.rem(x + offset, NX)

    def at_z(offset):
        return lax.rem(z + offset + NZ, NZ)

    def seq_of(xx, zz):
        return {"seq": xx * NZ + zz}

    barrier = pltpu.get_barrier_semaphore()
    partners = [seq_of(at_x(d), z) for d in range(1, NX)]
    partners += [seq_of(x, at_z(1)), seq_of(x, at_z(-1))]
    for partner in partners:
        pl.semaphore_signal(barrier, inc=1, device_id=partner, device_id_type=pl.DeviceIdType.MESH)
    pl.semaphore_wait(barrier, len(partners))

    kv = (kv_first, kv_second)

    def kv_rows(h, item, zz, xx):
        return kv[h].at[item, pl.ds(zz * UNITS + xx * SPANS, SPANS)]

    def kv_source(h, item, xx):
        source = (keys, values)[item]
        first = pl.multiple_of(xx * (KVH * HEAD_DIM) + h * HEAD_DIM, HEAD_DIM)
        return source.at[:, :, pl.ds(first, HEAD_DIM)]

    def x_copy(h, item, d):
        return pltpu.make_async_remote_copy(
            src_ref=kv_source(h, item, at_x(d)),
            dst_ref=kv_rows(h, item, z, x),
            send_sem=x_send.at[h, item, d - 1],
            recv_sem=x_recv.at[h, item, x],
            device_id=seq_of(at_x(d), z),
            device_id_type=pl.DeviceIdType.MESH,
        )

    def x_own(h, item):
        return pltpu.make_async_copy(
            kv_source(h, item, x), kv_rows(h, item, z, x), x_recv.at[h, item, x]
        )

    def q_source(h, xx):
        return queries.at[:, pl.ds(pl.multiple_of(xx * QW + h * GW, GW), GW)]

    def q_copy(h, d):
        return pltpu.make_async_remote_copy(
            src_ref=q_source(h, at_x(d)),
            dst_ref=q_buf.at[h, x],
            send_sem=q_send.at[h, d - 1],
            recv_sem=q_recv.at[h, x],
            device_id=seq_of(at_x(d), z),
            device_id_type=pl.DeviceIdType.MESH,
        )

    def q_own(h):
        return pltpu.make_async_copy(q_source(h, x), q_buf.at[h, x], q_recv.at[h, x])

    for h in range(KVH):
        for item in range(2):
            for d in (2, 1, 3):
                x_copy(h, item, d).start()
            x_own(h, item).start()
    for h in range(KVH):
        for d in (2, 1, 3):
            q_copy(h, d).start()
        q_own(h).start()

    def piece(h, item, half, zz):
        return kv[h].at[item, pl.ds(zz * UNITS + half * HALF, HALF)]

    def z_copy(h, way, hop, item, half):
        turn = 1 - 2 * way
        ref = piece(h, item, half, at_z(-turn * (hop - 1)))
        return pltpu.make_async_remote_copy(
            src_ref=ref,
            dst_ref=ref,
            send_sem=z_send.at[h, way, hop - 1, item, half],
            recv_sem=z_recv.at[h, way, hop - 1, item, half],
            device_id=seq_of(x, at_z(turn)),
            device_id_type=pl.DeviceIdType.MESH,
        )

    def z_arrived(h, way, hop, item, half):
        turn = 1 - 2 * way
        ref = piece(h, item, half, at_z(-turn * hop))
        pltpu.make_async_copy(ref, ref, z_recv.at[h, way, hop - 1, item, half]).wait()

    def z_first(h):
        for item in range(2):
            for half in range(2):
                for xx in (2 * half, 2 * half + 1):
                    ref = kv_rows(h, item, z, xx)
                    pltpu.make_async_copy(ref, ref, x_recv.at[h, item, xx]).wait()
                for way in range(2):
                    z_copy(h, way, 1, item, half).start()

    def z_forward(h, e):
        late = e // 8
        hop = 1 + e // 4
        item = (1 - late) * ((e % 4) // 2) + late * (e % 2)
        for way in range(2):
            half = (1 - late) * (e % 2) + late * way
            z_arrived(h, way, hop, item, half)
            z_copy(h, way, hop + 1, item, half).start()

    def z_last(h):
        for item in range(2):
            for way in range(2):
                z_arrived(h, way, 3, item, 1 - way)
        for item in range(2):
            for way in range(2):
                z_arrived(h, way, 4, item, way)

    def unit_of(u):
        d = lax.rem(lax.rem(u, NX) + 1, NX)
        return d, u // NX

    def span_of(u):
        d, s = unit_of(u)
        return order[(at_x(d) * NZ + z) * SPANS + s]

    z_first(0)

    def find_starts(u, carry):
        span = span_of(u)
        token = span * BLOCK + lax.broadcasted_iota(jnp.int32, (BLOCK, HEAD_DIM), 0)
        start = jnp.zeros((BLOCK, HEAD_DIM), jnp.int32)
        end = jnp.int32(0)
        for j in range(NDOC):
            end = end + lengths[j]
            start = jnp.where(token >= end, end, start)
        starts[u] = start - (span - PAD) * BLOCK
        return carry

    lax.fori_loop(0, UNITS, find_starts, 0)
    loader_k[0:PAD] = jnp.zeros((PAD, BLOCK, HEAD_DIM), jnp.bfloat16)
    loader_v[0:PAD] = jnp.zeros((PAD, BLOCK, HEAD_DIM), jnp.bfloat16)

    def forward_step(e, carry):
        z_forward(0, e)
        return carry

    lax.fori_loop(0, FORWARDS, forward_step, 0)
    z_first(1)

    for h in range(KVH):
        for xx in range(NX):
            pltpu.make_async_copy(q_buf.at[h, xx], q_buf.at[h, xx], q_recv.at[h, xx]).wait()

    lane = lax.broadcasted_iota(jnp.int32, (GROUP * BLOCK, 128), 1)
    row = lax.rem(lax.broadcasted_iota(jnp.int32, (GROUP * BLOCK, 128), 0), BLOCK)

    def o_rows(s, h, xx):
        return out.at[
            pl.ds(pl.multiple_of(s * BLOCK, BLOCK), BLOCK),
            pl.ds(pl.multiple_of(xx * QW + h * GW, GW), GW),
        ]

    def o_source(h, d, s):
        return o_buf.at[h, d, pl.ds(pl.multiple_of(s * BLOCK, BLOCK), BLOCK), :]

    def o_copy(h, d, s):
        return pltpu.make_async_remote_copy(
            src_ref=o_source(h, d, s),
            dst_ref=o_rows(s, h, x),
            send_sem=o_send.at[h, d, s],
            recv_sem=o_recv.at[h, d, s],
            device_id=seq_of(at_x(d), z),
            device_id_type=pl.DeviceIdType.MESH,
        )

    def o_own(h, s):
        return pltpu.make_async_copy(o_source(h, 0, s), o_rows(s, h, x), o_recv.at[h, 0, s])

    def send_unit(h, u):
        d, s = unit_of(u)

        @pl.when(d > 0)
        def _():
            o_copy(h, d, s).start()

        @pl.when(d == 0)
        def _():
            o_own(h, s).start()

    def attend(h, u):
        d, s = unit_of(u)
        xx = at_x(d)
        first = pl.multiple_of(s * BLOCK, BLOCK)
        q_rows = q_buf[h, xx, pl.ds(first, BLOCK), :]
        q = jnp.concatenate([q_rows[:, g * HEAD_DIM : (g + 1) * HEAD_DIM] for g in range(GROUP)], 0)
        span = span_of(u)
        window_k = jnp.concatenate([loader_k[span + n] for n in range(WIN)], 0)
        window_v = jnp.concatenate([loader_v[span + n] for n in range(WIN)], 0)
        scores = lax.dot_general(
            q, window_k, (((1,), (1,)), ((), ())), preferred_element_type=jnp.float32
        )
        start = starts[u]
        start = jnp.concatenate([start] * GROUP, 0)
        parts = []
        for c in range(WIN // 2):
            allowed = lane >= start - 128 * c
            if c == WIN // 2 - 1:
                allowed = allowed & (lane - BLOCK <= row)
            parts.append(jnp.where(allowed, scores[:, c * 128 : (c + 1) * 128], -jnp.inf))
        top = parts[0]
        for part in parts[1:]:
            top = jnp.maximum(top, part)
        top = jnp.max(top, axis=1, keepdims=True)
        parts = [jnp.exp2((part - top) * SCALE) for part in parts]
        total = parts[0]
        for part in parts[1:]:
            total = total + part
        total = jnp.sum(total, axis=1, keepdims=True)
        rounded = jnp.concatenate([part.astype(jnp.bfloat16) for part in parts], 1)
        mixed = jnp.dot(rounded, window_v, preferred_element_type=jnp.float32)
        mixed = (mixed / total).astype(jnp.bfloat16)
        for g in range(GROUP):
            o_buf[h, d, pl.ds(first, BLOCK), g * HEAD_DIM : (g + 1) * HEAD_DIM] = mixed[
                g * BLOCK : (g + 1) * BLOCK
            ]

    def to_loader(h):
        def move(i, carry):
            for n in range(4):
                t = 4 * i + n
                loader_k[PAD + t] = kv[h][0, places[t]]
                loader_v[PAD + t] = kv[h][1, places[t]]
            return carry

        lax.fori_loop(0, NSPAN // 4, move, 0)

    for h in range(KVH):
        z_last(h)
        to_loader(h)

        def unit_step(u, carry):
            if h == 0:

                @pl.when(u < FORWARDS)
                def _():
                    z_forward(1, u)

            attend(h, u)

            @pl.when(u > 0)
            def _():
                send_unit(h, u - 1)

            return carry

        lax.fori_loop(0, UNITS, unit_step, 0)
        send_unit(h, UNITS - 1)

    for h in range(KVH):
        for s in range(SPANS):
            o_own(h, s).wait()
            for d in range(1, NX):
                o_copy(h, d, s).wait_send()
                ref = o_rows(s, h, at_x(NX - d))
                pltpu.make_async_copy(ref, ref, o_recv.at[h, d, s]).wait()
    for h in range(KVH):
        for d in range(1, NX):
            for item in range(2):
                x_copy(h, item, d).wait_send()
            q_copy(h, d).wait_send()
        for item in range(2):
            for way in range(2):
                for half in range(2):
                    for hop in range(1, 5 if half == way else 4):
                        z_copy(h, way, hop, item, half).wait_send()


def shards(queries, keys, values, lengths, span_order):
    spans = jnp.arange(NSPAN, dtype=jnp.int32)
    holder = spans // SPANS
    place = ((holder % NZ) * NX + holder // NZ) * SPANS + spans % SPANS
    places = jnp.sum(jnp.where(span_order[:, None] == spans[None, :], place[:, None], 0), axis=0)
    smem = pl.BlockSpec(memory_space=pltpu.SMEM)
    anywhere = pl.BlockSpec(memory_space=pl.ANY)
    dma = pltpu.SemaphoreType.DMA
    return pl.pallas_call(
        body,
        out_shape=jax.ShapeDtypeStruct((ROWS, HEADS * HEAD_DIM), jnp.bfloat16),
        in_specs=[smem, smem, smem, anywhere, anywhere, anywhere],
        out_specs=anywhere,
        scratch_shapes=[
            pltpu.VMEM((2, NSPAN, BLOCK, HEAD_DIM), jnp.bfloat16),
            pltpu.VMEM((2, NSPAN, BLOCK, HEAD_DIM), jnp.bfloat16),
            pltpu.VMEM((PAD + NSPAN, BLOCK, HEAD_DIM), jnp.bfloat16),
            pltpu.VMEM((PAD + NSPAN, BLOCK, HEAD_DIM), jnp.bfloat16),
            pltpu.VMEM((KVH, NX, ROWS, GW), jnp.bfloat16),
            pltpu.VMEM((KVH, NX, ROWS, GW), jnp.bfloat16),
            pltpu.VMEM((UNITS, BLOCK, HEAD_DIM), jnp.int32),
            dma((KVH, 2, NX - 1)),
            dma((KVH, 2, NX)),
            dma((KVH, NX - 1)),
            dma((KVH, NX)),
            dma((KVH, 2, 4, 2, 2)),
            dma((KVH, 2, 4, 2, 2)),
            dma((KVH, NX, SPANS)),
            dma((KVH, NX, SPANS)),
        ],
        compiler_params=pltpu.CompilerParams(collective_id=0, has_side_effects=True),
        name="span_attention",
    )(
        lengths, span_order, places.astype(jnp.int32), queries,
        keys.reshape(SPANS, BLOCK, KV_HEADS * HEAD_DIM),
        values.reshape(SPANS, BLOCK, KV_HEADS * HEAD_DIM),
    )


def solution(mesh):
    placed = (
        P(("dp", "seq"), None),
        P(("dp", "seq"), None),
        P(("dp", "seq"), None),
        P("dp"),
        P("dp"),
    )
    return jax.shard_map(
        shards, mesh=mesh, in_specs=placed, out_specs=P(("dp", "seq"), None), check_vma=False
    )
```

time: 369 us -> 123 us (0.33)
  waiting for transfers between devices: 133 us -> 0 us
  Pallas kernels: 0 us -> 118 us
  matrix products: 69.9 us -> 0 us
  local copies, waits for them, and re-layouts: 60.3 us -> 3.13 us
  blocking collectives: 56.9 us -> 0 us
  starting transfers between devices: 25.8 us -> 0 us
  loops' own time: 11.6 us -> 0 us
  other arithmetic: 8.5 us -> 1.29 us
    all_to_all x3 -> x0, waiting for transfers between devices: 133 us -> none  [the longest x1 48.9 us: shards(): lax.all_to_all(wide_keys, 'seq', split_axis=1, concat_axis=0, tiled=True)]
    pallas_call x0 -> x1, Pallas kernels: none -> 118 us  [shards(): pl.pallas_call(body, out_shape=jax.ShapeDtypeStruct((ROWS, HEADS * HEAD_D...]
    dot_general x32 -> x0, matrix products: 69.9 us -> none  [the longest x16 43.1 us: one_block(): jnp.einsum('qgd,kd->gqk', query_block, key_block[:, 0], preferred_element...]
    all_to_all x1 -> x0, blocking collectives: 56.9 us -> none  [shards(): lax.all_to_all(balanced_out, 'seq', split_axis=0, concat_axis=1, tiled=True)]
    all_to_all x3 -> x0, starting transfers between devices: 25.8 us -> none  [the longest x1 13.2 us: shards(): lax.all_to_all(wide_keys, 'seq', split_axis=1, concat_axis=0, tiled=True)]
    dynamic_slice x48 -> x0, local copies, waits for them, and re-layouts: 13.1 us -> none  [the longest x16 10.6 us: attend(): lax.map(one_block, jnp.arange(total_rows // QBLOCK, dtype=jnp.int32))]
    dynamic_update_slice x32 -> x0, local copies, waits for them, and re-layouts: 12.6 us -> none  [attend(): lax.map(one_block, jnp.arange(total_rows // QBLOCK, dtype=jnp.int32))]
    another operation x1 -> x0, loops' own time: 11.6 us -> none  [attend(): lax.map(one_block, jnp.arange(total_rows // QBLOCK, dtype=jnp.int32))]
  transfers between devices with their start and end apart: 3 -> 0, of which waited for: 3 -> 0; matrix products, arithmetic and copies ran while one was open for 4% -> 0% of each run, Pallas kernels for 0% -> 0%
where the time goes in v1:
time: 123 us
  Pallas kernels  118 us (96%)
  local copies, waits for them, and re-layouts  3.13 us (3%)
  other arithmetic  1.29 us (1%)
    pallas_call x1, Pallas kernels, shards(): pl.pallas_call(body, out_shape=jax.ShapeDtypeStruct((ROWS, HEADS * HEAD_D...  118 us
    unnamed x1, local copies, waits for them, and re-layouts  3.13 us

profile of v1, /device:TPU:56, one launch (start us, length us, event | category | flops | bytes accessed | tf_op | source)
XLA Modules:
  0.0 122.7 jit_solution(7442078342721989772)
XLA Ops:
  0.0 1.3 %select_reduce_fusion.places = s32[128]{0:T(128)} fusion(s32[128]{0:T(128)S(1)} %fusion, s32[128]{0:T(128)} %order.1), kind=kLoop, calls=%fused_computation | loop fusion | flops 49024 | bytes 1536 | tf_op jit(solution)/shard_map/reduce_sum | solution.py:319
  1.3 118.3 %span_attention.1 = bf16[256,4096]{1,0:T(8,128)(2,1)} custom-call(s32[32]{0:T(128)} %lengths.1, s32[128]{0:T(128)} %order.1, s32[128]{0:T(128)} %select_reduce_fusion.places, bf16[256,4096]{1,0:T(8,128)(2,1)} %queries.1, bf16[4,64,1024]{2,1,0:T(8,128)(2,1)} %bitcast.2, bf16[4,64,1024]{2,1,0:T(8,128)(2,1)} %bitcast.3), custom_call_target="tpu_custom_call" | custom-call | tf_op jit(solution)/shard_map/span_attention/pallas_call | solution.py:323
  119.6 3.1 %copy.7 = bf16[256,4096]{1,0:T(8,128)(2,1)} copy(bf16[256,4096]{1,0:T(8,128)(2,1)} %span_attention.1) | data formatting | bytes 4194304
  (1 shorter events, 0.0 us)

commit v2 on v1

v2 whole, which is shorter than its diff:
```python
import functools
import math

import jax
import jax.numpy as jnp
from jax import lax
from jax.experimental import pallas as pl
from jax.experimental.pallas import tpu as pltpu
from jax.sharding import PartitionSpec as P

HEADS = 32
KV_HEADS = 8
HEAD_DIM = 128
BLOCK = 64
NX = 4
NZ = 8
ROWS = 256
SPANS = ROWS // BLOCK
GROUP = HEADS // KV_HEADS
KVH = KV_HEADS // NX
QW = HEADS * HEAD_DIM // NX
GW = GROUP * HEAD_DIM
TOKENS = NX * NZ * ROWS
NSPAN = TOKENS // BLOCK
PAD = 17
WIN = 18
UNITS = NX * SPANS
HALF = UNITS // 2
NDOC = 32
SCALE = HEAD_DIM**-0.5 * math.log2(math.e)


def body(
    lengths, order, places, queries, keys, values, out,
    k_first, v_first, k_second, v_second, q_buf, o_buf, starts, scores, weights, totals,
    x_send, x_recv, q_send, q_recv, z_send, z_recv, o_send, o_recv,
):
    me = lax.axis_index("seq")
    x = me // NZ
    z = lax.rem(me, NZ)
    kv = ((k_first, v_first), (k_second, v_second))

    def at_x(offset):
        return lax.rem(x + offset, NX)

    def at_z(offset):
        return lax.rem(z + offset + NZ, NZ)

    def seq_of(xx, zz):
        return {"seq": xx * NZ + zz}

    def send(src_ref, dst_ref, send_sem, recv_sem, target):
        return pltpu.make_async_remote_copy(
            src_ref=src_ref,
            dst_ref=dst_ref,
            send_sem=send_sem,
            recv_sem=recv_sem,
            device_id=target,
            device_id_type=pl.DeviceIdType.MESH,
        )

    def arrived(ref, sem):
        pltpu.make_async_copy(ref, ref, sem).wait()

    barrier = pltpu.get_barrier_semaphore()
    partners = [seq_of(at_x(d), z) for d in range(1, NX)]
    partners += [seq_of(x, at_z(1)), seq_of(x, at_z(-1))]
    for partner in partners:
        pl.semaphore_signal(barrier, inc=1, device_id=partner, device_id_type=pl.DeviceIdType.MESH)
    pl.semaphore_wait(barrier, len(partners))

    def kv_rows(h, item, d):
        return kv[h][item].at[pl.ds(z * UNITS + d * SPANS, SPANS)]

    def kv_source(h, item, d):
        first = pl.multiple_of(at_x(d) * (KVH * HEAD_DIM) + h * HEAD_DIM, HEAD_DIM)
        return (keys, values)[item].at[:, :, pl.ds(first, HEAD_DIM)]

    def x_copy(h, item, d):
        source, target, sem = kv_source(h, item, d), kv_rows(h, item, d), x_recv.at[h, item, d]
        if d == 0:
            return pltpu.make_async_copy(source, target, sem)
        return send(source, target, x_send.at[h, item, d], sem, seq_of(at_x(d), z))

    def q_copy(h, d):
        source = queries.at[:, pl.ds(pl.multiple_of(at_x(d) * QW + h * GW, GW), GW)]
        target, sem = q_buf.at[h, d], q_recv.at[h, d]
        if d == 0:
            return pltpu.make_async_copy(source, target, sem)
        return send(source, target, q_send.at[h, d], sem, seq_of(at_x(d), z))

    for h in range(KVH):
        for item in range(2):
            for d in range(NX):
                x_copy(h, item, d).start()
        for d in range(NX):
            q_copy(h, d).start()

    def piece(h, item, half, zz):
        return kv[h][item].at[pl.ds(zz * UNITS + half * HALF, HALF)]

    def z_copy(h, item, way, hop, half):
        turn = 1 - 2 * way
        ref = piece(h, item, half, at_z(-turn * (hop - 1)))
        sems = (h, item, way, hop - 1, half)
        return send(ref, ref, z_send.at[sems], z_recv.at[sems], seq_of(x, at_z(turn)))

    def z_arrived(h, item, way, hop, half):
        ref = piece(h, item, half, at_z((2 * way - 1) * hop))
        arrived(ref, z_recv.at[h, item, way, hop - 1, half])

    def z_start(h, item):
        for half in range(2):
            for d in (2 * half, 2 * half + 1):
                arrived(kv_rows(h, item, d), x_recv.at[h, item, d])
            for way in range(2):
                z_copy(h, item, way, 1, half).start()

    def z_forward(h, item, hop, half):
        for way in range(2):
            part = half if hop < 4 else way
            z_arrived(h, item, way, hop - 1, part)
            z_copy(h, item, way, hop, part).start()

    def z_forward_both(h, item, hop):
        for half in range(2):
            z_forward(h, item, hop, half)

    def z_finish(h, item):
        for way in range(2):
            z_arrived(h, item, way, 3, 1 - way)
        for way in range(2):
            z_arrived(h, item, way, 4, way)

    def unit_of(u):
        d = lax.rem(lax.rem(u, NX) + 1, NX)
        return d, u // NX

    def span_of(u):
        d, s = unit_of(u)
        return order[(at_x(d) * NZ + z) * SPANS + s]

    def run_units(step, events=()):
        def unit_step(u, carry):
            for when, event in events:
                pl.when(u == when)(event)
            step(u)
            return carry

        lax.fori_loop(0, UNITS, unit_step, 0)

    def find_starts(u):
        span = span_of(u)
        token = span * BLOCK + lax.broadcasted_iota(jnp.int32, (BLOCK, HEAD_DIM), 0)
        start = jnp.zeros((BLOCK, HEAD_DIM), jnp.int32)
        end = jnp.int32(0)
        for j in range(NDOC):
            end = end + lengths[j]
            start = jnp.where(token >= end, end, start)
        starts[u] = start - (span - PAD) * BLOCK

    lane = lax.broadcasted_iota(jnp.int32, (BLOCK, 128), 1)
    row = lax.broadcasted_iota(jnp.int32, (BLOCK, 128), 0)

    def window_of(h, item, u):
        span = span_of(u)
        return jnp.concatenate([kv[h][item][places[span + n]] for n in range(WIN)], 0)

    def weigh(h, u):
        d, s = unit_of(u)
        q_rows = q_buf[h, lax.rem(NX - d, NX), pl.ds(pl.multiple_of(s * BLOCK, BLOCK), BLOCK), :]
        q = jnp.concatenate([q_rows[:, g * HEAD_DIM : (g + 1) * HEAD_DIM] for g in range(GROUP)], 0)
        keys_here = window_of(h, 0, u)
        start = starts[u]
        tops = [jnp.full((BLOCK, 128), -jnp.inf, jnp.float32)] * GROUP
        for first in range(0, WIN * BLOCK, 256):
            width = min(256, WIN * BLOCK - first)
            block = lax.dot_general(
                q, keys_here[first : first + width], (((1,), (1,)), ((), ())),
                preferred_element_type=jnp.float32,
            )
            for c in range(0, width, 128):
                allowed = lane + (first + c) >= start
                if first + c + 128 == WIN * BLOCK:
                    allowed = allowed & (lane - BLOCK <= row)
                for g in range(GROUP):
                    part = block[g * BLOCK : (g + 1) * BLOCK, c : c + 128]
                    part = jnp.where(allowed, part, -jnp.inf)
                    tops[g] = jnp.maximum(tops[g], part)
                    scores[(first + c) // 128, g * BLOCK : (g + 1) * BLOCK, :] = part
        for g in range(GROUP):
            rows = slice(g * BLOCK, (g + 1) * BLOCK)
            top = jnp.max(tops[g], axis=1, keepdims=True)
            total = jnp.zeros((BLOCK, 128), jnp.float32)
            for c in range(WIN // 2):
                part = jnp.exp2((scores[c, rows, :] - top) * SCALE)
                total = total + part
                weights[u, c, rows, :] = part.astype(jnp.bfloat16)
            total = jnp.sum(total, axis=1, keepdims=True)
            totals[u, rows, :] = jnp.broadcast_to(total, (BLOCK, HEAD_DIM))

    def o_rows(h, xx, s):
        return out.at[
            pl.ds(pl.multiple_of(s * BLOCK, BLOCK), BLOCK),
            pl.ds(pl.multiple_of(xx * QW + h * GW, GW), GW),
        ]

    def o_source(h, d, s):
        return o_buf.at[h, d, pl.ds(pl.multiple_of(s * BLOCK, BLOCK), BLOCK), :]

    def o_copy(h, d, s):
        sem = o_recv.at[h, d, s]
        return send(o_source(h, d, s), o_rows(h, x, s), o_send.at[h, d, s], sem, seq_of(at_x(d), z))

    def o_own(h, s):
        return pltpu.make_async_copy(o_source(h, 0, s), o_rows(h, x, s), o_recv.at[h, 0, s])

    def send_unit(h, u):
        d, s = unit_of(u)

        @pl.when(d > 0)
        def _():
            o_copy(h, d, s).start()

        @pl.when(d == 0)
        def _():
            o_own(h, s).start()

    def mix(h, u):
        d, s = unit_of(u)
        rounded = jnp.concatenate([weights[u, c] for c in range(WIN // 2)], 1)
        mixed = jnp.dot(rounded, window_of(h, 1, u), preferred_element_type=jnp.float32)
        mixed = (mixed / totals[u]).astype(jnp.bfloat16)
        for g in range(GROUP):
            o_buf[
                h, d, pl.ds(pl.multiple_of(s * BLOCK, BLOCK), BLOCK),
                g * HEAD_DIM : (g + 1) * HEAD_DIM,
            ] = mixed[g * BLOCK : (g + 1) * BLOCK]

        @pl.when(u > 0)
        def _():
            send_unit(h, u - 1)

    def q_wait(h):
        for d in range(NX):
            arrived(q_buf.at[h, d], q_recv.at[h, d])

    def forward(*step):
        return lambda: z_forward(*step)

    z_start(0, 0)
    run_units(find_starts)
    z_forward_both(0, 0, 2)
    z_forward_both(0, 0, 3)
    z_start(0, 1)
    z_forward(0, 0, 4, 0)
    z_forward_both(0, 1, 2)
    z_finish(0, 0)
    q_wait(0)
    run_units(
        functools.partial(weigh, 0),
        [(1, forward(0, 1, 3, 0)), (4, forward(0, 1, 3, 1)), (5, lambda: z_start(1, 0))],
    )
    z_forward(0, 1, 4, 0)
    z_forward_both(1, 0, 2)
    z_finish(0, 1)
    run_units(
        functools.partial(mix, 0),
        [(4, forward(1, 0, 3, 0)), (8, forward(1, 0, 3, 1)), (9, lambda: z_start(1, 1))],
    )
    send_unit(0, UNITS - 1)
    z_forward(1, 0, 4, 0)
    z_forward_both(1, 1, 2)
    z_finish(1, 0)
    q_wait(1)
    run_units(
        functools.partial(weigh, 1),
        [(4, forward(1, 1, 3, 0)), (8, forward(1, 1, 3, 1)), (12, forward(1, 1, 4, 0))],
    )
    z_finish(1, 1)
    run_units(functools.partial(mix, 1))
    send_unit(1, UNITS - 1)

    for h in range(KVH):
        for s in range(SPANS):
            o_own(h, s).wait()
            for d in range(1, NX):
                o_copy(h, d, s).wait_send()
                arrived(o_rows(h, at_x(NX - d), s), o_recv.at[h, d, s])
    for h in range(KVH):
        for d in range(1, NX):
            for item in range(2):
                x_copy(h, item, d).wait_send()
            q_copy(h, d).wait_send()
        for item in range(2):
            for way in range(2):
                for half in range(2):
                    for hop in range(1, 5 if half == way else 4):
                        z_copy(h, item, way, hop, half).wait_send()


def shards(queries, keys, values, lengths, span_order):
    spans = jnp.arange(NSPAN, dtype=jnp.int32)
    holder = spans // SPANS
    x = lax.axis_index("seq") // NZ
    slot = (x - holder // NZ + NX) % NX
    place = ((holder % NZ) * NX + slot) * SPANS + spans % SPANS
    padded = jnp.arange(-PAD, NSPAN, dtype=jnp.int32)
    places = jnp.sum(jnp.where(span_order[:, None] == padded[None, :], place[:, None], 0), axis=0)
    smem = pl.BlockSpec(memory_space=pltpu.SMEM)
    anywhere = pl.BlockSpec(memory_space=pl.ANY)
    dma = pltpu.SemaphoreType.DMA
    return pl.pallas_call(
        body,
        out_shape=jax.ShapeDtypeStruct((ROWS, HEADS * HEAD_DIM), jnp.bfloat16),
        in_specs=[smem, smem, smem, anywhere, anywhere, anywhere],
        out_specs=anywhere,
        scratch_shapes=[
            *[pltpu.VMEM((NSPAN, BLOCK, HEAD_DIM), jnp.bfloat16)] * (2 * KVH),
            pltpu.VMEM((KVH, NX, ROWS, GW), jnp.bfloat16),
            pltpu.VMEM((KVH, NX, ROWS, GW), jnp.bfloat16),
            pltpu.VMEM((UNITS, BLOCK, HEAD_DIM), jnp.int32),
            pltpu.VMEM((WIN // 2, GROUP * BLOCK, 128), jnp.float32),
            pltpu.VMEM((UNITS, WIN // 2, GROUP * BLOCK, 128), jnp.bfloat16),
            pltpu.VMEM((UNITS, GROUP * BLOCK, HEAD_DIM), jnp.float32),
            dma((KVH, 2, NX)),
            dma((KVH, 2, NX)),
            dma((KVH, NX)),
            dma((KVH, NX)),
            dma((KVH, 2, 2, 4, 2)),
            dma((KVH, 2, 2, 4, 2)),
            dma((KVH, NX, SPANS)),
            dma((KVH, NX, SPANS)),
        ],
        compiler_params=pltpu.CompilerParams(collective_id=0, has_side_effects=True),
        name="span_attention",
    )(
        lengths, span_order, places.astype(jnp.int32), queries,
        keys.reshape(SPANS, BLOCK, KV_HEADS * HEAD_DIM),
        values.reshape(SPANS, BLOCK, KV_HEADS * HEAD_DIM),
    )


def solution(mesh):
    placed = (
        P(("dp", "seq"), None),
        P(("dp", "seq"), None),
        P(("dp", "seq"), None),
        P("dp"),
        P("dp"),
    )
    return jax.shard_map(
        shards, mesh=mesh, in_specs=placed, out_specs=P(("dp", "seq"), None), check_vma=False
    )
```

time: 123 us -> 115 us (0.935)
  Pallas kernels: 118 us -> 110 us
    pallas_call x1, Pallas kernels: 118 us -> 110 us  [shards(): pl.pallas_call(body, out_shape=jax.ShapeDtypeStruct((ROWS, HEADS * HEAD_D...]
where the time goes in v2:
time: 115 us
  Pallas kernels  110 us (96%)
  local copies, waits for them, and re-layouts  3.13 us (3%)
  other arithmetic  1.44 us (1%)
    pallas_call x1, Pallas kernels, shards(): pl.pallas_call(body, out_shape=jax.ShapeDtypeStruct((ROWS, HEADS * HEAD_D...  110 us
    unnamed x1, local copies, waits for them, and re-layouts  3.13 us

profile of v2, /device:TPU:56, one launch (start us, length us, event | category | flops | bytes accessed | tf_op | source)
XLA Modules:
  0.0 115.1 jit_solution(7632684166335703642)
XLA Ops:
  0.0 1.4 %select_reduce_fusion.places = s32[145]{0:T(256)} fusion(s32[128]{0:T(128)S(1)} %fusion, s32[128]{0:T(128)} %order.1, s32[145]{0:T(256)S(1)} %iota_add_fusion), kind=kLoop, calls=%fused_computation | loop fusion | flops 55535 | bytes 2184 | tf_op jit(solution)/shard_map/reduce_sum | solution.py:309
  1.4 110.5 %span_attention.1 = bf16[256,4096]{1,0:T(8,128)(2,1)} custom-call(s32[32]{0:T(128)} %lengths.1, s32[128]{0:T(128)} %order.1, s32[145]{0:T(256)} %select_reduce_fusion.places, bf16[256,4096]{1,0:T(8,128)(2,1)} %queries.1, bf16[4,64,1024]{2,1,0:T(8,128)(2,1)} %bitcast.2, bf16[4,64,1024]{2,1,0:T(8,128)(2,1)} %bitcast.3), custom_call_target="tpu_custom_call" | custom-call | tf_op jit(solution)/shard_map/span_attention/pallas_call | solution.py:313
  111.9 3.1 %copy.7 = bf16[256,4096]{1,0:T(8,128)(2,1)} copy(bf16[256,4096]{1,0:T(8,128)(2,1)} %span_attention.1) | data formatting | bytes 4194304
  (2 shorter events, 0.0 us)

commit v3 on v2

--- a/solution.py
+++ b/solution.py
@@ -33,7 +33,7 @@
 def body(
     lengths, order, places, queries, keys, values, out,
     k_first, v_first, k_second, v_second, q_buf, o_buf, starts, scores, weights, totals,
-    x_send, x_recv, q_send, q_recv, z_send, z_recv, o_send, o_recv,
+    x_send, x_recv, q_send, q_recv, own_send, own_recv, z_send, z_recv, o_send, o_recv,
 ):
     me = lax.axis_index("seq")
     x = me // NZ
@@ -69,15 +69,15 @@
         pl.semaphore_signal(barrier, inc=1, device_id=partner, device_id_type=pl.DeviceIdType.MESH)
     pl.semaphore_wait(barrier, len(partners))
 
-    def kv_rows(h, item, d):
-        return kv[h][item].at[pl.ds(z * UNITS + d * SPANS, SPANS)]
+    def kv_rows(h, item, zz, d):
+        return kv[h][item].at[pl.ds(zz * UNITS + d * SPANS, SPANS)]
 
     def kv_source(h, item, d):
         first = pl.multiple_of(at_x(d) * (KVH * HEAD_DIM) + h * HEAD_DIM, HEAD_DIM)
         return (keys, values)[item].at[:, :, pl.ds(first, HEAD_DIM)]
 
     def x_copy(h, item, d):
-        source, target, sem = kv_source(h, item, d), kv_rows(h, item, d), x_recv.at[h, item, d]
+        source, target, sem = kv_source(h, item, d), kv_rows(h, item, z, d), x_recv.at[h, item, d]
         if d == 0:
             return pltpu.make_async_copy(source, target, sem)
         return send(source, target, x_send.at[h, item, d], sem, seq_of(at_x(d), z))
@@ -102,19 +102,26 @@
     def z_copy(h, item, way, hop, half):
         turn = 1 - 2 * way
         ref = piece(h, item, half, at_z(-turn * (hop - 1)))
-        sems = (h, item, way, hop - 1, half)
+        sems = (h, item, way, hop - 2, half)
         return send(ref, ref, z_send.at[sems], z_recv.at[sems], seq_of(x, at_z(turn)))
 
+    def z_own(h, item, way, d):
+        ref, sems = kv_rows(h, item, z, d), (h, item, way, d)
+        return send(ref, ref, own_send.at[sems], own_recv.at[sems], seq_of(x, at_z(1 - 2 * way)))
+
     def z_arrived(h, item, way, hop, half):
-        ref = piece(h, item, half, at_z((2 * way - 1) * hop))
-        arrived(ref, z_recv.at[h, item, way, hop - 1, half])
+        source = at_z((2 * way - 1) * hop)
+        if hop > 1:
+            arrived(piece(h, item, half, source), z_recv.at[h, item, way, hop - 2, half])
+        else:
+            for d in (2 * half, 2 * half + 1):
+                arrived(kv_rows(h, item, source, d), own_recv.at[h, item, way, d])
 
     def z_start(h, item):
-        for half in range(2):
-            for d in (2 * half, 2 * half + 1):
-                arrived(kv_rows(h, item, d), x_recv.at[h, item, d])
+        for d in range(NX):
+            arrived(kv_rows(h, item, z, d), x_recv.at[h, item, d])
             for way in range(2):
-                z_copy(h, item, way, 1, half).start()
+                z_own(h, item, way, d).start()
 
     def z_forward(h, item, hop, half):
         for way in range(2):
@@ -294,8 +301,10 @@
             q_copy(h, d).wait_send()
         for item in range(2):
             for way in range(2):
+                for d in range(NX):
+                    z_own(h, item, way, d).wait_send()
                 for half in range(2):
-                    for hop in range(1, 5 if half == way else 4):
+                    for hop in range(2, 5 if half == way else 4):
                         z_copy(h, item, way, hop, half).wait_send()
 
 
@@ -312,9 +321,9 @@
     dma = pltpu.SemaphoreType.DMA
     return pl.pallas_call(
         body,
-        out_shape=jax.ShapeDtypeStruct((ROWS, HEADS * HEAD_DIM), jnp.bfloat16),
+        out_shape=pltpu.VMEM((ROWS, HEADS * HEAD_DIM), jnp.bfloat16),
         in_specs=[smem, smem, smem, anywhere, anywhere, anywhere],
-        out_specs=anywhere,
+        out_specs=pl.BlockSpec(memory_space=pltpu.VMEM),
         scratch_shapes=[
             *[pltpu.VMEM((NSPAN, BLOCK, HEAD_DIM), jnp.bfloat16)] * (2 * KVH),
             pltpu.VMEM((KVH, NX, ROWS, GW), jnp.bfloat16),
@@ -327,12 +336,16 @@
             dma((KVH, 2, NX)),
             dma((KVH, NX)),
             dma((KVH, NX)),
-            dma((KVH, 2, 2, 4, 2)),
-            dma((KVH, 2, 2, 4, 2)),
+            dma((KVH, 2, 2, NX)),
+            dma((KVH, 2, 2, NX)),
+            dma((KVH, 2, 2, 3, 2)),
+            dma((KVH, 2, 2, 3, 2)),
             dma((KVH, NX, SPANS)),
             dma((KVH, NX, SPANS)),
         ],
-        compiler_params=pltpu.CompilerParams(collective_id=0, has_side_effects=True),
+        compiler_params=pltpu.CompilerParams(
+            collective_id=0, has_side_effects=True, vmem_limit_bytes=58 * 2**20
+        ),
         name="span_attention",
     )(
         lengths, span_order, places.astype(jnp.int32), queries,

time: 115 us -> 113 us (0.983)
  local copies, waits for them, and re-layouts: 3.13 us -> 1.32 us
    unnamed x1, local copies, waits for them, and re-layouts: 3.13 us -> 1.32 us
where the time goes in v3:
time: 113 us
  Pallas kernels  110 us (97%)
  other arithmetic  1.44 us (1%)
  local copies, waits for them, and re-layouts  1.32 us (1%)
    pallas_call x1, Pallas kernels, shards(): pl.pallas_call(body, out_shape=pltpu.VMEM((ROWS, HEADS * HEAD_DIM), jnp.b...  110 us

profile of v3, /device:TPU:56, one launch (start us, length us, event | category | flops | bytes accessed | tf_op | source)
XLA Modules:
  0.0 113.0 jit_solution(5455916240257085699)
XLA Ops:
  0.0 1.4 %select_reduce_fusion.places = s32[145]{0:T(256)} fusion(s32[128]{0:T(128)S(1)} %fusion, s32[128]{0:T(128)} %order.1, s32[145]{0:T(256)S(1)} %iota_add_fusion), kind=kLoop, calls=%fused_computation | loop fusion | flops 55535 | bytes 2184 | tf_op jit(solution)/shard_map/reduce_sum | solution.py:318
  1.4 110.2 %span_attention.1 = bf16[256,4096]{1,0:T(8,128)(2,1)S(1)} custom-call(s32[32]{0:T(128)} %lengths.1, s32[128]{0:T(128)} %order.1, s32[145]{0:T(256)} %select_reduce_fusion.places, bf16[256,4096]{1,0:T(8,128)(2,1)} %queries.1, bf16[4,64,1024]{2,1,0:T(8,128)(2,1)} %bitcast.2, bf16[4,64,1024]{2,1,0:T(8,128)(2,1)} %bitcast.3), custom_call_target="tpu_custom_call" | custom-call | tf_op jit(solution)/shard_map/span_attention/pallas_call | solution.py:322
  111.6 1.3 %copy.7 = bf16[256,4096]{1,0:T(8,128)(2,1)} copy(bf16[256,4096]{1,0:T(8,128)(2,1)S(1)} %span_attention.1) | data formatting | bytes 4194304
  (2 shorter events, 0.0 us)

commit v4 on v3

--- a/solution.py
+++ b/solution.py
@@ -31,8 +31,8 @@
 
 
 def body(
-    lengths, order, places, queries, keys, values, out,
-    k_first, v_first, k_second, v_second, q_buf, o_buf, starts, scores, weights, totals,
+    lengths, order, order_row, queries, keys, values, out,
+    k_first, v_first, k_second, v_second, q_buf, o_buf, places, starts, scores, weights, totals,
     x_send, x_recv, q_send, q_recv, own_send, own_recv, z_send, z_recv, o_send, o_recv,
 ):
     me = lax.axis_index("seq")
@@ -140,12 +140,26 @@
             z_arrived(h, item, way, 4, way)
 
     def unit_of(u):
-        d = lax.rem(lax.rem(u, NX) + 1, NX)
-        return d, u // NX
+        turn = lax.rem(u, NX)
+        return lax.rem(1 + 2 * turn + turn // 2, NX), u // NX
 
     def span_of(u):
         d, s = unit_of(u)
         return order[(at_x(d) * NZ + z) * SPANS + s]
+
+    def find_places(part):
+        span = lax.broadcasted_iota(jnp.int32, (1, NSPAN), 1)
+        slot = (x - span // (SPANS * NZ) + NX) & (NX - 1)
+        place = ((span // SPANS) & (NZ - 1)) * UNITS + slot * SPANS + (span & (SPANS - 1))
+        loader = order_row[...]
+
+        def some(i, carry):
+            for n in range(8):
+                t = (4 * part + i) * 8 + n
+                places[PAD + t] = jnp.max(jnp.where(loader == t, place, 0))
+            return carry
+
+        lax.fori_loop(0, 4, some, 0)
 
     def run_units(step, events=()):
         def unit_step(u, carry):
@@ -256,12 +270,18 @@
         return lambda: z_forward(*step)
 
     z_start(0, 0)
-    run_units(find_starts)
+    for n in range(PAD):
+        places[n] = 0
+    find_places(0)
     z_forward_both(0, 0, 2)
+    find_places(1)
     z_forward_both(0, 0, 3)
     z_start(0, 1)
+    find_places(2)
     z_forward(0, 0, 4, 0)
+    run_units(find_starts)
     z_forward_both(0, 1, 2)
+    find_places(3)
     z_finish(0, 0)
     q_wait(0)
     run_units(
@@ -309,25 +329,20 @@
 
 
 def shards(queries, keys, values, lengths, span_order):
-    spans = jnp.arange(NSPAN, dtype=jnp.int32)
-    holder = spans // SPANS
-    x = lax.axis_index("seq") // NZ
-    slot = (x - holder // NZ + NX) % NX
-    place = ((holder % NZ) * NX + slot) * SPANS + spans % SPANS
-    padded = jnp.arange(-PAD, NSPAN, dtype=jnp.int32)
-    places = jnp.sum(jnp.where(span_order[:, None] == padded[None, :], place[:, None], 0), axis=0)
     smem = pl.BlockSpec(memory_space=pltpu.SMEM)
+    vmem = pl.BlockSpec(memory_space=pltpu.VMEM)
     anywhere = pl.BlockSpec(memory_space=pl.ANY)
     dma = pltpu.SemaphoreType.DMA
     return pl.pallas_call(
         body,
         out_shape=pltpu.VMEM((ROWS, HEADS * HEAD_DIM), jnp.bfloat16),
-        in_specs=[smem, smem, smem, anywhere, anywhere, anywhere],
-        out_specs=pl.BlockSpec(memory_space=pltpu.VMEM),
+        in_specs=[smem, smem, vmem, anywhere, anywhere, anywhere],
+        out_specs=vmem,
         scratch_shapes=[
             *[pltpu.VMEM((NSPAN, BLOCK, HEAD_DIM), jnp.bfloat16)] * (2 * KVH),
             pltpu.VMEM((KVH, NX, ROWS, GW), jnp.bfloat16),
             pltpu.VMEM((KVH, NX, ROWS, GW), jnp.bfloat16),
+            pltpu.SMEM((PAD + NSPAN,), jnp.int32),
             pltpu.VMEM((UNITS, BLOCK, HEAD_DIM), jnp.int32),
             pltpu.VMEM((WIN // 2, GROUP * BLOCK, 128), jnp.float32),
             pltpu.VMEM((UNITS, WIN // 2, GROUP * BLOCK, 128), jnp.bfloat16),
@@ -348,7 +363,7 @@
         ),
         name="span_attention",
     )(
-        lengths, span_order, places.astype(jnp.int32), queries,
+        lengths, span_order, span_order.reshape(1, NSPAN), queries,
         keys.reshape(SPANS, BLOCK, KV_HEADS * HEAD_DIM),
         values.reshape(SPANS, BLOCK, KV_HEADS * HEAD_DIM),
     )

time: 113 us -> 112 us (level)
  other arithmetic: 1.44 us -> 0 us
    reduce_sum x1 -> x0, other arithmetic: 1.41 us -> none  [shards(): jnp.sum(jnp.where(span_order[:, None] == padded[None, :], place[:, None],...]
where the time goes in v4:
time: 112 us
  Pallas kernels  110 us (98%)
  local copies, waits for them, and re-layouts  1.32 us (1%)
    pallas_call x1, Pallas kernels, shards(): pl.pallas_call(body, out_shape=pltpu.VMEM((ROWS, HEADS * HEAD_DIM), jnp.b...  110 us

profile of v4, /device:TPU:56, one launch (start us, length us, event | category | flops | bytes accessed | tf_op | source)
XLA Modules:
  0.0 111.6 jit_solution(9160370104642210641)
XLA Ops:
  0.0 110.2 %span_attention.1 = bf16[256,4096]{1,0:T(8,128)(2,1)S(1)} custom-call(s32[32]{0:T(128)} %lengths.1, s32[128]{0:T(128)} %order.1, s32[1,128]{1,0:T(1,128)} %bitcast.5, bf16[256,4096]{1,0:T(8,128)(2,1)} %queries.1, bf16[4,64,1024]{2,1,0:T(8,128)(2,1)} %bitcast.3, bf16[4,64,1024]{2,1,0:T(8,128)(2,1)} %bitcast.4), custom_call_target="tpu_custom_call" | custom-call | tf_op jit(solution)/shard_map/span_attention/pallas_call | solution.py:336
  110.2 1.3 %copy.7 = bf16[256,4096]{1,0:T(8,128)(2,1)} copy(bf16[256,4096]{1,0:T(8,128)(2,1)S(1)} %span_attention.1) | data formatting | bytes 4194304

commit v5 on v4

--- a/solution.py
+++ b/solution.py
@@ -125,7 +125,8 @@
 
     def z_forward(h, item, hop, half):
         for way in range(2):
-            part = half if hop < 4 else way
+            lead = way if (h, item) == (1, 1) else 0
+            part = way if hop == 4 else (half + lead) % 2
             z_arrived(h, item, way, hop - 1, part)
             z_copy(h, item, way, hop, part).start()
 
@@ -302,7 +303,7 @@
     q_wait(1)
     run_units(
         functools.partial(weigh, 1),
-        [(4, forward(1, 1, 3, 0)), (8, forward(1, 1, 3, 1)), (12, forward(1, 1, 4, 0))],
+        [(4, forward(1, 1, 3, 0)), (7, forward(1, 1, 3, 1)), (11, forward(1, 1, 4, 0))],
     )
     z_finish(1, 1)
     run_units(functools.partial(mix, 1))

time: 112 us -> 112 us (level)
  no operation moved by 1% of the time
where the time goes in v5:
time: 112 us
  Pallas kernels  110 us (98%)
  local copies, waits for them, and re-layouts  1.32 us (1%)
    pallas_call x1, Pallas kernels, shards(): pl.pallas_call(body, out_shape=pltpu.VMEM((ROWS, HEADS * HEAD_DIM), jnp.b...  110 us

profile of v5, /device:TPU:56, one launch (start us, length us, event | category | flops | bytes accessed | tf_op | source)
XLA Modules:
  0.0 111.6 jit_solution(9515759705382946813)
XLA Ops:
  0.0 110.2 %span_attention.1 = bf16[256,4096]{1,0:T(8,128)(2,1)S(1)} custom-call(s32[32]{0:T(128)} %lengths.1, s32[128]{0:T(128)} %order.1, s32[1,128]{1,0:T(1,128)} %bitcast.5, bf16[256,4096]{1,0:T(8,128)(2,1)} %queries.1, bf16[4,64,1024]{2,1,0:T(8,128)(2,1)} %bitcast.3, bf16[4,64,1024]{2,1,0:T(8,128)(2,1)} %bitcast.4), custom_call_target="tpu_custom_call" | custom-call | tf_op jit(solution)/shard_map/span_attention/pallas_call | solution.py:337
  110.2 1.3 %copy.7 = bf16[256,4096]{1,0:T(8,128)(2,1)} copy(bf16[256,4096]{1,0:T(8,128)(2,1)S(1)} %span_attention.1) | data formatting | bytes 4194304
